TPU v7x, 32 devices: a whole 2x2x4 slice. The times are simulated.
32 devices in a mesh: dp: 4 (over y, core), space: 4 (over z), tensor: 2 (over x).
Axes of the slice: x: 2, y: 2, z: 4, core: 2. Of those that a mesh axis runs over, the one named last changes fastest.
Arguments:
- feature_map: bfloat16 [4, 32, 48, 1536], P('dp', 'space', None, 'tensor'), may hold values from -12 to 12
- conv_kernel: float32 [7, 7, 1536], replicated, may hold values from -6 to 6
- conv_bias: float32 [1536], replicated, may hold values from -4 to 4
- norm_gain: float32 [1536], replicated, may hold values from 0.1 to 1.9
- norm_bias: float32 [1536], replicated, may hold values from -3 to 3
- expand_weight: bfloat16 [1536, 6144], P(None, 'tensor'), may hold values from -0.21875 to 0.21875
- expand_bias: float32 [6144], P('tensor'), may hold values from -3 to 3
- project_weight: bfloat16 [6144, 1536], P('tensor'), may hold values from -0.109375 to 0.109375
- project_bias: float32 [1536], P('tensor'), may hold values from -3 to 3
- layer_scale: float32 [1536], P('tensor'), may hold values from 0.3 to 1.5
- cotangent: bfloat16 [4, 32, 48, 1536], P('dp', 'space', None, 'tensor'), may hold values from -6 to 6
Outputs:
- block_out: bfloat16 [4, 32, 48, 1536], P('dp', 'space', None, 'tensor')
- grad_input: bfloat16 [4, 32, 48, 1536], P('dp', 'space', None, 'tensor')
- grad_expand: float32 [1536, 6144], P(None, 'tensor')
- grad_project: float32 [6144, 1536], P('tensor')
- grad_kernel: float32 [7, 7, 1536], P(None, None, 'tensor')
All inputs are finite; a program needn't handle non-finite values.
Results may differ from a plain program's by a relative error of at most 0.0067.
Values may be sent and summed in bfloat16 or wider, within the bound.
A program may use at most 192 MiB of HBM per device.

v0:
```python
import jax
import jax.numpy as jnp
from jax import lax
from jax.sharding import PartitionSpec as P

EPSILON = 1e-06
INV_ROOT_TWO = 0.7071067811865476
INV_ROOT_TAU = 0.3989422804014327


def padded_2(block, sides, width):
    for axis, dim in sides:
        count = lax.axis_size(axis)
        forward = [(i, i + 1) for i in range(count - 1)]
        backward = [(target, source) for source, target in forward]
        low = lax.ppermute(
            lax.slice_in_dim(block, block.shape[dim] - width, None, axis=dim), axis, forward
        )
        high = lax.ppermute(lax.slice_in_dim(block, 0, width, axis=dim), axis, backward)
        block = jnp.concatenate([low, block, high], axis=dim)
    return block


def row_rims(block_data):
    return padded_2(block_data, (("space", 1),), 3)


def all_channels(block_data):
    return lax.all_gather(block_data, "tensor", axis=1, tiled=True)


def channel_total(stacked):
    return lax.psum(stacked, "tensor")


def partial_sums(term_rows):
    return lax.psum_scatter(term_rows, "tensor", scatter_dimension=1, tiled=True)


def pixel_total(term, dim):
    shared = lax.psum_scatter(term, ("dp", "space"), scatter_dimension=dim, tiled=True)
    whole = lax.all_gather(shared.astype(jnp.bfloat16), ("dp", "space"), axis=dim, tiled=True)
    return whole.astype(jnp.float32)


def depthwise(padded, tap_weights, row_count, col_count):
    widened = jnp.pad(padded.astype(jnp.float32), ((0, 0), (0, 0), (3, 3), (0, 0)))
    running = jnp.zeros((widened.shape[0], row_count, col_count, widened.shape[3]), jnp.float32)
    for tap_row in range(7):
        for tap_col in range(7):
            running = (
                running
                + tap_weights[tap_row, tap_col]
                * widened[:, tap_row : tap_row + row_count, tap_col : tap_col + col_count, :]
            )
    return running


def kernel_grad(grad_block, padded, row_count, col_count):
    widened = jnp.pad(padded.astype(jnp.float32), ((0, 0), (0, 0), (3, 3), (0, 0)))
    grad_float = grad_block.astype(jnp.float32)
    tap_rows = []
    for tap_row in range(7):
        tap_line = []
        for tap_col in range(7):
            window = widened[:, tap_row : tap_row + row_count, tap_col : tap_col + col_count, :]
            tap_line.append(jnp.sum(grad_float * window, axis=(0, 1, 2)))
        tap_rows.append(jnp.stack(tap_line))
    return jnp.stack(tap_rows)


def gelu_slope(values):
    cumulative = 0.5 * (1.0 + lax.erf(values * INV_ROOT_TWO))
    density = jnp.exp(-0.5 * values * values) * INV_ROOT_TAU
    return cumulative + values * density


def body(
    feature_map,
    conv_kernel,
    conv_bias,
    norm_gain,
    norm_bias,
    expand_weight,
    expand_bias,
    project_weight,
    project_bias,
    layer_scale,
    cotangent,
):
    images, row_count, col_count, shard_width = feature_map.shape
    pixels = images * row_count * col_count
    full_width = expand_weight.shape[0]
    offset = lax.axis_index("tensor") * shard_width
    own_gain = lax.dynamic_slice_in_dim(norm_gain, offset, shard_width, 0)
    own_kernel = lax.dynamic_slice_in_dim(conv_kernel, offset, shard_width, 2)
    padded = row_rims(feature_map)
    own_bias = lax.dynamic_slice_in_dim(conv_bias, offset, shard_width, 0)
    own_shift = lax.dynamic_slice_in_dim(norm_bias, offset, shard_width, 0)
    filtered = (depthwise(padded, own_kernel, row_count, col_count) + own_bias).reshape(
        pixels, shard_width
    )
    average = channel_total(jnp.sum(filtered, axis=1)) / full_width
    centered = filtered - average[:, None]
    spread = channel_total(jnp.sum(centered * centered, axis=1)) / full_width
    inverse = lax.rsqrt(spread + EPSILON)[:, None]
    unit_norm = centered * inverse
    gathered = all_channels((unit_norm * own_gain + own_shift).astype(jnp.bfloat16))
    hidden = jnp.dot(gathered, expand_weight, preferred_element_type=jnp.float32) + expand_bias
    activated = jax.nn.gelu(hidden, approximate=False).astype(jnp.bfloat16)
    projected = partial_sums(jnp.dot(activated, project_weight, preferred_element_type=jnp.float32))
    residual = feature_map.reshape(pixels, shard_width).astype(jnp.float32)
    block_out = (
        (residual + layer_scale * (projected + project_bias))
        .astype(jnp.bfloat16)
        .reshape(feature_map.shape)
    )
    grad_scaled = (cotangent.reshape(pixels, shard_width).astype(jnp.float32) * layer_scale).astype(
        jnp.bfloat16
    )
    grad_full = all_channels(grad_scaled)
    grad_project = pixel_total(
        lax.dot_general(
            activated, grad_full, (((0,), (0,)), ((), ())), preferred_element_type=jnp.float32
        ),
        1,
    )
    grad_act = lax.dot_general(
        grad_full, project_weight, (((1,), (1,)), ((), ())), preferred_element_type=jnp.float32
    )
    grad_hidden = (grad_act * gelu_slope(hidden)).astype(jnp.bfloat16)
    grad_expand = pixel_total(
        lax.dot_general(
            gathered, grad_hidden, (((0,), (0,)), ((), ())), preferred_element_type=jnp.float32
        ),
        0,
    )
    normed_terms = lax.dot_general(
        grad_hidden, expand_weight, (((1,), (1,)), ((), ())), preferred_element_type=jnp.float32
    )
    grad_normed = partial_sums(normed_terms)
    scaled_grad = grad_normed * own_gain
    channel_means = (
        lax.psum(
            jnp.stack([jnp.sum(scaled_grad, axis=1), jnp.sum(scaled_grad * unit_norm, axis=1)]),
            "tensor",
        )
        / full_width
    )
    grad_filtered = (
        (scaled_grad - channel_means[0][:, None] - unit_norm * channel_means[1][:, None]) * inverse
    ).astype(jnp.bfloat16)
    grad_block = grad_filtered.reshape(images, row_count, col_count, shard_width)
    grad_kernel = kernel_grad(grad_block, padded, row_count, col_count)
    grad_padded = row_rims(grad_block)
    grad_input = (
        cotangent.astype(jnp.float32)
        + depthwise(grad_padded, own_kernel[::-1, ::-1], row_count, col_count)
    ).astype(jnp.bfloat16)
    grad_kernel = lax.psum(grad_kernel, ("dp", "space"))
    return (block_out, grad_input, grad_expand, grad_project, grad_kernel)


def solution(mesh):
    in_specs = (
        P("dp", "space", None, "tensor"),
        P(),
        P(),
        P(),
        P(),
        P(None, "tensor"),
        P("tensor"),
        P("tensor", None),
        P("tensor"),
        P("tensor"),
        P("dp", "space", None, "tensor"),
    )
    out_specs = (
        P("dp", "space", None, "tensor"),
        P("dp", "space", None, "tensor"),
        P(None, "tensor"),
        P("tensor", None),
        P(None, None, "tensor"),
    )
    return jax.shard_map(body, mesh=mesh, in_specs=in_specs, out_specs=out_specs, check_vma=False)
```

profile of v0, /device:TPU:1, one launch (start us, length us, event | category | flops | bytes accessed | tf_op | source)
XLA Modules:
  0.0 874.0 jit_solution(9765757772026388206)
XLA Ops:
  7.2 0.0 all-gather.5.cloned.1.call-start
  7.2 1.1 fusion.175
  8.4 4.0 collective-permute-start
  12.4 1.3 collective-permute-start.1
  13.7 0.8 dynamic_slice.14
  14.5 0.8 dynamic_slice.13
  15.2 0.8 dynamic_slice.15
  16.0 2.4 fusion.161
  18.5 1.8 collective-permute-done.1
  20.3 0.2 maximum_convert_fusion
  20.5 12.7 %fusion.173 = (f32[8,48]{1,0:T(8,128)S(1)}, f32[1,8,48,768]{3,2,1,0:T(8,128)S(1)}) fusion(f32[768]{0:T(1024)S(1)} %dynamic_slice.13, f32[768]{0:T(1024)S(1)} %get-tuple-element.109, f32[768]{0:T(1024)S(1)} %get-tuple-element.62, f32[768]{0:T(1024)S(1)} %get-tuple-element.63, f32[1,14,48,768]{3,2,1,0:T(8,128)S(1)} %maximum_convert_fusion, ...), kind=kLoop, calls=%fused_computation.396 | loop fusion | flops 29195904 | bytes 11707904 | tf_op jit(solution)/shard_map/reduce_sum | solution.py:103
  33.2 0.1 reduce_sum.482
  33.3 3.8 psum.28
  37.1 0.1 sub.30
  37.1 0.3 multiply_reduce_fusion.1
  37.4 0.1 reduce_sum.484
  37.5 3.8 psum.29
  41.3 1.1 add_convert_fusion
  42.3 0.0 all-gather.5.cloned.1.call-update
  42.4 0.0 reduce-scatter.5.cloned.1.call-start
  42.4 26.4 %all-gather.5.cloned.1.call-done = bf16[384,1536]{1,0:T(8,128)(2,1)} async-done(((bf16[384,768]{1,0:T(8,128)(2,1)}), bf16[384,1536]{1,0:T(8,128)(2,1)}) %all-gather.5.cloned.1.call-update) | async-done | bytes 1179664 | tf_op jit(solution)/shard_map/all_gather | solution.py:29
  68.8 17.0 %fusion.2 = (bf16[384,3072]{1,0:T(8,128)(2,1)S(1)}, f32[384,3072]{1,0:T(8,128)}) fusion(f32[3072]{0:T(1024)S(1)} %copy-done.10, bf16[384,1536]{1,0:T(8,128)(2,1)} %all-gather.5.cloned.1.call-done, bf16[1536,3072]{1,0:T(8,128)(2,1)} %param.16), kind=kOutput, calls=%fused_computation.53 | convolution fusion | flops 3701735424 | bytes 17707008 | tf_op jit(solution)/shard_map/dot_general | solution.py:109
  85.8 1.4 copy-done.3
  87.1 7.7 fusion.176
  94.9 0.0 reduce-scatter.5.cloned.1.call-update
  94.9 0.0 all-gather.7.cloned.1.call-start
  95.0 34.9 %reduce-scatter.5.cloned.1.call-done = f32[384,768]{1,0:T(8,128)} async-done(((f32[384,1536]{1,0:T(8,128)}), f32[384,768]{1,0:T(8,128)}) %reduce-scatter.5.cloned.1.call-update) | async-done | bytes 1179664 | tf_op jit(solution)/shard_map/reduce_scatter | solution.py:37
  129.8 2.9 fusion.158
  132.7 0.2 reduce-scatter.9.cloned.1.call-start
  133.0 22.7 %all-gather.7.cloned.1.call-done = bf16[384,1536]{1,0:T(8,128)(2,1)} async-done(((bf16[384,768]{1,0:T(8,128)(2,1)}), bf16[384,1536]{1,0:T(8,128)(2,1)}) %all-gather.7.cloned.1.call-update) | async-done | bytes 1179664 | tf_op jit(solution)/shard_map/all_gather | solution.py:29
  155.7 8.4 fusion.8
  164.0 1.4 copy-done.4
  165.5 9.5 %fusion.178 = f32[1536,3072]{1,0:T(8,128)} fusion(bf16[384,1536]{1,0:T(8,128)(2,1)S(1)} %copy-done.6, bf16[384,3072]{1,0:T(8,128)(2,1)S(1)} %fusion.8), kind=kOutput, calls=%fused_computation.401 | convolution fusion | flops 3623878656 | bytes 22413312 | tf_op jit(solution)/shard_map/dot_general | solution.py:133
  175.0 0.0 reduce-scatter.11.cloned.1.call-start
  175.0 13.7 %fusion.179 = f32[3072,1536]{0,1:T(8,128)} fusion(bf16[384,3072]{1,0:T(8,128)(2,1)} %copy-done.3, bf16[384,1536]{1,0:T(8,128)(2,1)} %all-gather.7.cloned.1.call-done), kind=kOutput, calls=%fused_computation.402 | convolution fusion | flops 3623878656 | bytes 22413312 | tf_op jit(solution)/shard_map/dot_general | solution.py:123
  188.8 0.0 reduce-scatter.7.cloned.1.call-start
  188.8 12.0 %fusion.177 = f32[384,1536]{1,0:T(8,128)} fusion(bf16[384,3072]{1,0:T(8,128)(2,1)} %copy-done.4, bf16[1536,3072]{1,0:T(8,128)(2,1)} %param.16), kind=kOutput, calls=%fused_computation.400 | convolution fusion | flops 3623878656 | bytes 14155776 | tf_op jit(solution)/shard_map/dot_general | solution.py:138
  200.8 0.0 all-gather.9.cloned.1.call-start
  200.9 168.3 %reduce-scatter.9.cloned.1.call-done = f32[96,3072]{1,0:T(8,128)} async-done(((f32[1536,3072]{1,0:T(8,128)}), f32[96,3072]{1,0:T(8,128)}) %reduce-scatter.9.cloned.1.call-update) | async-done | bytes 1179664 | tf_op jit(solution)/shard_map/reduce_scatter | solution.py:41
  369.2 2.2 convert_element_type.100
  371.4 0.0 all-gather.11.cloned.1.call-start
  371.4 195.5 %reduce-scatter.11.cloned.1.call-done = f32[3072,96]{0,1:T(8,128)} async-done(((f32[3072,1536]{0,1:T(8,128)}), f32[3072,96]{0,1:T(8,128)}) %reduce-scatter.11.cloned.1.call-update) | async-done | bytes 1179664 | tf_op jit(solution)/shard_map/reduce_scatter | solution.py:41
  566.9 2.2 convert_element_type.102
  569.1 0.0 all-reduce.4.cloned.1.call-start
  569.2 33.8 %reduce-scatter.7.cloned.1.call-done = f32[384,768]{1,0:T(8,128)} async-done(((f32[384,1536]{1,0:T(8,128)}), f32[384,768]{1,0:T(8,128)}) %reduce-scatter.7.cloned.1.call-update) | async-done | bytes 1179664 | tf_op jit(solution)/shard_map/reduce_scatter | solution.py:37
  602.9 1.7 multiply_reduce_fusion.2
  604.6 4.0 psum.30
  608.6 1.6 multiply_convert_fusion
  610.3 2.0 fusion.153
  612.5 2.9 fusion.154
  615.4 2.9 fusion.155
  618.8 3.2 collective-permute-start.2
  622.1 1.3 collective-permute-start.3
  623.8 0.7 copy-done.7
  624.5 6.9 collective-permute-done.2
  631.4 9.2 %collective-permute-done.3 = bf16[1,3,48,768]{3,2,1,0:T(8,128)(2,1)S(1)} collective-permute-done((bf16[1,3,48,768]{3,2,1,0:T(8,128)(2,1)S(1)}, bf16[1,3,48,768]{3,2,1,0:T(8,128)(2,1)S(1)}, u32[]{:S(2)}, u32[]{:S(2)}) %collective-permute-start.3) | collective-permute-done | bytes 221216 | tf_op jit(solution)/shard_map/ppermute | solution.py:19
  640.6 0.2 maximum_convert_fusion.1
  640.7 9.7 %fusion.104 = bf16[1,8,48,768]{3,2,1,0:T(8,128)(2,1)} fusion(f32[1,14,48,768]{3,2,1,0:T(8,128)S(1)} %maximum_convert_fusion.1, f32[768]{0:T(1024)S(1)} %get-tuple-element.109, f32[768]{0:T(1024)S(1)} %get-tuple-element.62, f32[768]{0:T(1024)S(1)} %get-tuple-element.63, f32[768]{0:T(1024)S(1)} %get-tuple-element.64, f32[768]{0:T(1024)S(1)} %get-tuple-element.65, ...), kind=kLoop, calls=%fused_computation.247 | loop fusion | flops 29491200 | bytes 11702272 | tf_op jit(solution)/shard_map/convert_element_type | solution.py:159
  650.4 41.7 %all-gather.9.cloned.1.call-done = bf16[1536,3072]{1,0:T(8,128)(2,1)} async-done(((bf16[96,3072]{1,0:T(8,128)(2,1)}), bf16[1536,3072]{1,0:T(8,128)(2,1)}) %all-gather.9.cloned.1.call-update) | async-done | bytes 9437200 | tf_op jit(solution)/shard_map/all_gather | solution.py:42
  692.1 12.7 %convert_element_type.101 = f32[1536,3072]{1,0:T(8,128)} convert(bf16[1536,3072]{1,0:T(8,128)(2,1)} %all-gather.9.cloned.1.call-done) | non-fusion elementwise | flops 4718592 | bytes 28311552 | tf_op jit(solution)/shard_map/convert_element_type | solution.py:43
  704.8 68.9 %all-gather.11.cloned.1.call-done = bf16[3072,1536]{0,1:T(8,128)(2,1)} async-done(((bf16[3072,96]{0,1:T(8,128)(2,1)}), bf16[3072,1536]{0,1:T(8,128)(2,1)}) %all-gather.11.cloned.1.call-update) | async-done | bytes 9437200 | tf_op jit(solution)/shard_map/all_gather | solution.py:42
  773.7 13.5 %copy.16 = f32[3072,1536]{1,0:T(8,128)} copy(bf16[3072,1536]{0,1:T(8,128)(2,1)} %all-gather.11.cloned.1.call-done) | data formatting | bytes 28311552
  787.3 78.6 %all-reduce.4.cloned.1.call-done = f32[7,7,768]{2,1,0:T(8,128)} async-done(((f32[7,7,768]{2,1,0:T(8,128)}), f32[7,7,768]{2,1,0:T(8,128)}) %all-reduce.4.cloned.1.call-update) | async-done | bytes 150544 | tf_op jit(solution)/shard_map/psum | solution.py:160
  865.9 1.6 copy.24
  (98 shorter events, 0.8 us)
Async XLA Ops:
  7.2 13.2 %copy-start.2 = (bf16[1,8,48,768]{3,2,1,0:T(8,128)(2,1)S(1)}, bf16[1,8,48,768]{3,2,1,0:T(8,128)(2,1)}, u32[]{:S(2)}) copy-start(bf16[1,8,48,768]{3,2,1,0:T(8,128)(2,1)} %param.11) | copy-start | bytes 1769476
  7.2 61.6 %all-gather.5.cloned.1.call-start = ((), (), s32[]{:S(2)}) async-start(), calls=%async_computation.4 | async-start | bytes 1769472 | tf_op jit(solution)/shard_map/all_gather | solution.py:29
  8.4 10.1 %collective-permute-start = (bf16[1,3,48,768]{3,2,1,0:T(8,128)(2,1)S(1)}, bf16[1,3,48,768]{3,2,1,0:T(8,128)(2,1)S(1)}, u32[]{:S(2)}, u32[]{:S(2)}) collective-permute-start(bf16[1,3,48,768]{3,2,1,0:T(8,128)(2,1)S(1)} %get-tuple-element.116), channel_id=1, source_target_pairs={{0,2},{2,4},{4,6},{1,3},{3,5},{5,7},{8,10},{10,12},{12,14},{9,11},... | collective-permute-start | bytes 663560 | tf_op jit(solution)/shard_map/ppermute | solution.py:16
  12.4 7.9 collective-permute-start.1
  41.3 27.5 %copy-start.10 = (f32[3072]{0:T(1024)S(1)}, f32[3072]{0:T(1024)}, u32[]{:S(2)}) copy-start(f32[3072]{0:T(1024)} %param.17) | copy-start | bytes 36868
  42.4 87.5 %reduce-scatter.5.cloned.1.call-start = ((), (), s32[]{:S(2)}) async-start(), calls=%async_computation.5 | async-start | bytes 3538944 | tf_op jit(solution)/shard_map/reduce_scatter | solution.py:37
  85.7 1.4 copy-start.3
  94.9 35.0 %copy-start.8 = (f32[768]{0:T(1024)S(1)}, f32[768]{0:T(1024)}, u32[]{:S(2)}) copy-start(f32[768]{0:T(1024)} %param.20) | copy-start | bytes 9220
  94.9 35.0 %copy-start.9 = (f32[768]{0:T(1024)S(1)}, f32[768]{0:T(1024)}, u32[]{:S(2)}) copy-start(f32[768]{0:T(1024)} %param.19) | copy-start | bytes 9220
  94.9 60.7 %all-gather.7.cloned.1.call-start = ((), (), s32[]{:S(2)}) async-start(), calls=%async_computation.6 | async-start | bytes 1769472 | tf_op jit(solution)/shard_map/all_gather | solution.py:29
  132.7 236.5 %reduce-scatter.9.cloned.1.call-start = ((), (), s32[]{:S(2)}) async-start(), calls=%async_computation.8 | async-start | bytes 20054016 | tf_op jit(solution)/shard_map/reduce_scatter | solution.py:41
  155.7 9.8 %copy-start.6 = (bf16[384,1536]{1,0:T(8,128)(2,1)S(1)}, bf16[384,1536]{1,0:T(8,128)(2,1)}, u32[]{:S(2)}) copy-start(bf16[384,1536]{1,0:T(8,128)(2,1)} %all-gather.5.cloned.1.call-done) | copy-start | bytes 3538948
  164.0 1.4 copy-start.4
  175.0 391.9 %reduce-scatter.11.cloned.1.call-start = ((), (), s32[]{:S(2)}) async-start(), calls=%async_computation.10 | async-start | bytes 20054016 | tf_op jit(solution)/shard_map/reduce_scatter | solution.py:41
  188.8 414.1 %reduce-scatter.7.cloned.1.call-start = ((), (), s32[]{:S(2)}) async-start(), calls=%async_computation.7 | async-start | bytes 3538944 | tf_op jit(solution)/shard_map/reduce_scatter | solution.py:37
  200.8 491.3 %all-gather.9.cloned.1.call-start = ((), (), s32[]{:S(2)}) async-start(), calls=%async_computation.9 | async-start | bytes 10027008 | tf_op jit(solution)/shard_map/all_gather | solution.py:42
  371.4 402.3 %all-gather.11.cloned.1.call-start = ((), (), s32[]{:S(2)}) async-start(), calls=%async_computation.11 | async-start | bytes 10027008 | tf_op jit(solution)/shard_map/all_gather | solution.py:42
  569.1 296.8 %all-reduce.4.cloned.1.call-start = ((), (), s32[]{:S(2)}) async-start(), calls=%async_computation.12 | async-start | bytes 344064 | tf_op jit(solution)/shard_map/psum | solution.py:160
  610.3 8.5 copy-start
  618.8 21.8 %copy-start.1 = (bf16[384,768]{1,0:T(8,128)(2,1)S(1)}, bf16[384,768]{1,0:T(8,128)(2,1)}, u32[]{:S(2)}) copy-start(bf16[384,768]{1,0:T(8,128)(2,1)} %copy-done) | copy-start | bytes 1769476
  618.8 12.5 %collective-permute-start.2 = (bf16[1,3,48,768]{3,2,1,0:T(8,128)(2,1)S(1)}, bf16[1,3,48,768]{3,2,1,0:T(8,128)(2,1)S(1)}, u32[]{:S(2)}, u32[]{:S(2)}) collective-permute-start(bf16[1,3,48,768]{3,2,1,0:T(8,128)(2,1)S(1)} %get-tuple-element.114), channel_id=1, source_target_pairs={{0,2},{2,4},{4,6},{1,3},{3,5},{5,7},{8,10},{10,12},{12,14},{9,11},... | collective-permute-start | bytes 663560 | tf_op jit(solution)/shard_map/ppermute | solution.py:16
  622.1 18.5 %collective-permute-start.3 = (bf16[1,3,48,768]{3,2,1,0:T(8,128)(2,1)S(1)}, bf16[1,3,48,768]{3,2,1,0:T(8,128)(2,1)S(1)}, u32[]{:S(2)}, u32[]{:S(2)}) collective-permute-start(bf16[1,3,48,768]{3,2,1,0:T(8,128)(2,1)S(1)} %get-tuple-element.115), channel_id=1, source_target_pairs={{2,0},{4,2},{6,4},{3,1},{5,3},{7,5},{10,8},{12,10},{14,12},{11,9},... | collective-permute-start | bytes 663560 | tf_op jit(solution)/shard_map/ppermute | solution.py:19
  623.8 0.7 copy-start.7
  624.5 16.2 %copy-start.5 = (bf16[1,8,48,768]{3,2,1,0:T(8,128)(2,1)S(1)}, bf16[1,8,48,768]{3,2,1,0:T(8,128)(2,1)}, u32[]{:S(2)}) copy-start(bf16[1,8,48,768]{3,2,1,0:T(8,128)(2,1)} %param.21) | copy-start | bytes 1769476
Sparse Core Ops, SparseCore 0:
  42.5 26.2 all-gather.4
  95.0 34.7 reduce-scatter.4
  132.9 22.7 all-gather.6
  175.1 194.0 reduce-scatter.8
  373.7 193.1 reduce-scatter.10
  569.0 33.8 reduce-scatter.6
  605.8 86.2 all-gather.8
  694.4 79.2 all-gather.10
  777.7 88.1 all-reduce.3
where the time goes:
time: 875 us; the launch traced here: 874 us
  waiting for transfers between devices  689 us (79%)
  matrix products  68.3 us (8%)
  other arithmetic  55.1 us (6%)
  local copies, waits for them, and re-layouts  25.4 us (3%)
  between operations  14.5 us (2%)
  blocking collectives  11.5 us (1%)
  starting transfers between devices  10.4 us (1%)
    reduce_scatter x2, waiting for transfers between devices, pixel_total(): lax.psum_scatter(term, ('dp', 'space'), scatter_dimension=dim, tiled=True)  364 us
    all_gather x2, waiting for transfers between devices, pixel_total(): lax.all_gather(shared.astype(jnp.bfloat16), ('dp', 'space'), axis=dim, ti...  111 us
    psum x1, waiting for transfers between devices, body(): grad_kernel = lax.psum(grad_kernel, ('dp', 'space'))  78.6 us
    reduce_scatter x2, waiting for transfers between devices, partial_sums(): lax.psum_scatter(term_rows, 'tensor', scatter_dimension=1, tiled=True)  68.6 us
    all_gather x2, waiting for transfers between devices, all_channels(): return lax.all_gather(block_data, 'tensor', axis=1, tiled=True)  49.1 us
    unnamed x30, local copies, waits for them, and re-layouts  18.7 us
  transfers between devices with their start and end apart: 13, of which 12 were waited for; matrix products, arithmetic and copies ran while one was open for 9% of the time, Pallas kernels for 0%

commit v1 on v0

--- a/solution.py
+++ b/solution.py
@@ -157,7 +157,7 @@
         cotangent.astype(jnp.float32)
         + depthwise(grad_padded, own_kernel[::-1, ::-1], row_count, col_count)
     ).astype(jnp.bfloat16)
-    grad_kernel = lax.psum(grad_kernel, ("dp", "space"))
+    grad_kernel = jnp.sum(lax.all_gather(grad_kernel, ("dp", "space")), axis=0)
     return (block_out, grad_input, grad_expand, grad_project, grad_kernel)
 
 

time: 875 us -> 836 us (0.955)
  waiting for transfers between devices: 689 us -> 655 us
    psum x1 -> x0, waiting for transfers between devices: 78.6 us -> none  [body(): grad_kernel = lax.psum(grad_kernel, ('dp', 'space'))]
    all_gather x2, waiting for transfers between devices: 111 us -> 149 us  [pixel_total(): lax.all_gather(shared.astype(jnp.bfloat16), ('dp', 'space'), axis=dim, ti...]
    all_gather x0 -> x1, waiting for transfers between devices: none -> 23.9 us  [body(): grad_kernel = jnp.sum(lax.all_gather(grad_kernel, ('dp', 'space')), axis=0)]
    reduce_scatter x2, waiting for transfers between devices: 68.6 us -> 47.1 us  [partial_sums(): lax.psum_scatter(term_rows, 'tensor', scatter_dimension=1, tiled=True)]
    reduce_scatter x2, waiting for transfers between devices: 364 us -> 377 us  [pixel_total(): lax.psum_scatter(term, ('dp', 'space'), scatter_dimension=dim, tiled=True)]
    unnamed x30 -> x27, local copies, waits for them, and re-layouts: 18.7 us -> 17.1 us
  transfers between devices with their start and end apart: 13 -> 13, of which waited for: 12 -> 12; matrix products, arithmetic and copies ran while one was open for 9% -> 8% of each run, Pallas kernels for 0% -> 0%
where the time goes in v1:
time: 836 us; the launch traced here: 835 us
  waiting for transfers between devices  655 us (78%)
  matrix products  63.3 us (8%)
  other arithmetic  57.8 us (7%)
  local copies, waits for them, and re-layouts  23.8 us (3%)
  between operations  14.5 us (2%)
  blocking collectives  11.5 us (1%)
  starting transfers between devices  9.08 us (1%)
    reduce_scatter x2, waiting for transfers between devices, pixel_total(): lax.psum_scatter(term, ('dp', 'space'), scatter_dimension=dim, tiled=True)  377 us
    all_gather x2, waiting for transfers between devices, pixel_total(): lax.all_gather(shared.astype(jnp.bfloat16), ('dp', 'space'), axis=dim, ti...  149 us
    all_gather x2, waiting for transfers between devices, all_channels(): return lax.all_gather(block_data, 'tensor', axis=1, tiled=True)  49.1 us
    reduce_scatter x2, waiting for transfers between devices, partial_sums(): lax.psum_scatter(term_rows, 'tensor', scatter_dimension=1, tiled=True)  47.1 us
    all_gather x1, waiting for transfers between devices, body(): grad_kernel = jnp.sum(lax.all_gather(grad_kernel, ('dp', 'space')), axis=0)  23.9 us
    unnamed x27, local copies, waits for them, and re-layouts  17.1 us
    dot_general x1, matrix products, body(): jnp.dot(gathered, expand_weight, preferred_element_type=jnp.float32)  17 us
  transfers between devices with their start and end apart: 13, of which 12 were waited for; matrix products, arithmetic and copies ran while one was open for 8% of the time, Pallas kernels for 0%

profile of v1, /device:TPU:1, one launch (start us, length us, event | category | flops | bytes accessed | tf_op | source)
XLA Modules:
  0.0 835.0 jit_solution(14128379969573443042)
XLA Ops:
  7.2 0.0 all-gather.7.cloned.1.call-start
  7.2 1.1 fusion.175
  8.4 4.0 collective-permute-start
  12.4 1.3 collective-permute-start.1
  13.7 0.8 dynamic_slice.14
  14.5 0.8 dynamic_slice.13
  15.2 0.8 dynamic_slice.15
  16.0 2.4 fusion.161
  18.5 1.8 collective-permute-done.1
  20.3 0.2 maximum_convert_fusion
  20.5 12.7 %fusion.173 = (f32[8,48]{1,0:T(8,128)S(1)}, f32[1,8,48,768]{3,2,1,0:T(8,128)S(1)}) fusion(f32[768]{0:T(1024)S(1)} %dynamic_slice.13, f32[768]{0:T(1024)S(1)} %get-tuple-element.114, f32[768]{0:T(1024)S(1)} %get-tuple-element.67, f32[768]{0:T(1024)S(1)} %get-tuple-element.68, f32[1,14,48,768]{3,2,1,0:T(8,128)S(1)} %maximum_convert_fusion, ...), kind=kLoop, calls=%fused_computation.396 | loop fusion | flops 29195904 | bytes 11707904 | tf_op jit(solution)/shard_map/reduce_sum | solution.py:103
  33.2 0.1 reduce_sum.491
  33.3 3.8 psum.21
  37.1 0.1 sub.30
  37.1 0.3 multiply_reduce_fusion.1
  37.4 0.1 reduce_sum.493
  37.5 3.8 psum.22
  41.3 1.1 add_convert_fusion
  42.3 0.0 all-gather.7.cloned.1.call-update
  42.4 0.0 reduce-scatter.5.cloned.1.call-start
  42.4 26.4 %all-gather.7.cloned.1.call-done = bf16[384,1536]{1,0:T(8,128)(2,1)} async-done(((bf16[384,768]{1,0:T(8,128)(2,1)}), bf16[384,1536]{1,0:T(8,128)(2,1)}) %all-gather.7.cloned.1.call-update) | async-done | bytes 1179664 | tf_op jit(solution)/shard_map/all_gather | solution.py:29
  68.8 17.0 %fusion.2 = (bf16[384,3072]{1,0:T(8,128)(2,1)S(1)}, f32[384,3072]{1,0:T(8,128)}) fusion(f32[3072]{0:T(1024)S(1)} %copy-done.9, bf16[384,1536]{1,0:T(8,128)(2,1)} %all-gather.7.cloned.1.call-done, bf16[1536,3072]{1,0:T(8,128)(2,1)} %param.16), kind=kOutput, calls=%fused_computation.53 | convolution fusion | flops 3701735424 | bytes 17707008 | tf_op jit(solution)/shard_map/dot_general | solution.py:109
  85.8 1.4 copy-done.3
  87.2 7.7 fusion.176
  94.9 0.0 reduce-scatter.5.cloned.1.call-update
  94.9 0.0 all-gather.9.cloned.1.call-start
  95.0 34.9 %reduce-scatter.5.cloned.1.call-done = f32[384,768]{1,0:T(8,128)} async-done(((f32[384,1536]{1,0:T(8,128)}), f32[384,768]{1,0:T(8,128)}) %reduce-scatter.5.cloned.1.call-update) | async-done | bytes 1179664 | tf_op jit(solution)/shard_map/reduce_scatter | solution.py:37
  129.9 2.9 fusion.158
  132.8 0.2 reduce-scatter.7.cloned.1.call-start
  133.0 22.7 %all-gather.9.cloned.1.call-done = bf16[384,1536]{1,0:T(8,128)(2,1)} async-done(((bf16[384,768]{1,0:T(8,128)(2,1)}), bf16[384,1536]{1,0:T(8,128)(2,1)}) %all-gather.9.cloned.1.call-update) | async-done | bytes 1179664 | tf_op jit(solution)/shard_map/all_gather | solution.py:29
  155.7 8.3 fusion.8
  164.0 1.4 copy-done.4
  165.4 7.8 fusion.177
  173.2 0.0 reduce-scatter.9.cloned.1.call-start
  173.3 11.1 %fusion.178 = f32[1536,3072]{1,0:T(8,128)} fusion(bf16[384,1536]{1,0:T(8,128)(2,1)} %all-gather.7.cloned.1.call-done, bf16[384,3072]{1,0:T(8,128)(2,1)} %copy-done.4), kind=kOutput, calls=%fused_computation.401 | convolution fusion | flops 3623878656 | bytes 22413312 | tf_op jit(solution)/shard_map/dot_general | solution.py:133
  184.4 0.0 reduce-scatter.11.cloned.1.call-start
  184.5 11.4 %fusion.179 = f32[3072,1536]{0,1:T(8,128)} fusion(bf16[384,3072]{1,0:T(8,128)(2,1)} %copy-done.3, bf16[384,1536]{1,0:T(8,128)(2,1)} %all-gather.9.cloned.1.call-done), kind=kOutput, calls=%fused_computation.402 | convolution fusion | flops 3623878656 | bytes 22413312 | tf_op jit(solution)/shard_map/dot_general | solution.py:123
  195.9 0.0 all-gather.15.cloned.1.call-start
  195.9 12.2 %reduce-scatter.7.cloned.1.call-done = f32[384,768]{1,0:T(8,128)} async-done(((f32[384,1536]{1,0:T(8,128)}), f32[384,768]{1,0:T(8,128)}) %reduce-scatter.7.cloned.1.call-update) | async-done | bytes 1179664 | tf_op jit(solution)/shard_map/reduce_scatter | solution.py:37
  208.1 1.7 multiply_reduce_fusion.2
  209.8 4.0 psum.23
  213.9 1.6 multiply_convert_fusion
  215.5 2.0 fusion.153
  217.7 2.9 fusion.154
  220.6 2.9 fusion.155
  224.4 0.7 copy-done.6
  225.1 0.0 all-gather.11.cloned.1.call-start
  225.2 181.7 %reduce-scatter.9.cloned.1.call-done = f32[96,3072]{1,0:T(8,128)} async-done(((f32[1536,3072]{1,0:T(8,128)}), f32[96,3072]{1,0:T(8,128)}) %reduce-scatter.9.cloned.1.call-update) | async-done | bytes 1179664 | tf_op jit(solution)/shard_map/reduce_scatter | solution.py:41
  406.8 2.2 convert_element_type.100
  409.0 0.0 all-gather.13.cloned.1.call-start
  409.1 195.5 %reduce-scatter.11.cloned.1.call-done = f32[3072,96]{0,1:T(8,128)} async-done(((f32[3072,1536]{0,1:T(8,128)}), f32[3072,96]{0,1:T(8,128)}) %reduce-scatter.11.cloned.1.call-update) | async-done | bytes 1179664 | tf_op jit(solution)/shard_map/reduce_scatter | solution.py:41
  604.6 2.2 convert_element_type.102
  606.8 1.8 collective-permute-start.2
  608.6 1.4 collective-permute-start.3
  610.0 2.4 collective-permute-done.2
  612.4 4.5 collective-permute-done.3
  616.9 0.2 maximum_convert_fusion.1
  617.1 9.7 %fusion.104 = bf16[1,8,48,768]{3,2,1,0:T(8,128)(2,1)} fusion(f32[1,14,48,768]{3,2,1,0:T(8,128)S(1)} %maximum_convert_fusion.1, f32[768]{0:T(1024)S(1)} %get-tuple-element.114, f32[768]{0:T(1024)S(1)} %get-tuple-element.67, f32[768]{0:T(1024)S(1)} %get-tuple-element.68, f32[768]{0:T(1024)S(1)} %get-tuple-element.69, f32[768]{0:T(1024)S(1)} %get-tuple-element.70, ...), kind=kLoop, calls=%fused_computation.247 | loop fusion | flops 29491200 | bytes 11702272 | tf_op jit(solution)/shard_map/convert_element_type | solution.py:159
  626.8 23.9 %all-gather.15.cloned.1.call-done = f32[112,7,768]{2,1,0:T(8,128)} async-done(((f32[7,7,768]{2,1,0:T(8,128)}), f32[112,7,768]{2,1,0:T(8,128)}) %all-gather.15.cloned.1.call-update) | async-done | bytes 2408464 | tf_op jit(solution)/shard_map/all_gather | solution.py:160
  650.7 2.6 reduce_sum.545
  653.3 80.0 %all-gather.11.cloned.1.call-done = bf16[1536,3072]{1,0:T(8,128)(2,1)} async-done(((bf16[96,3072]{1,0:T(8,128)(2,1)}), bf16[1536,3072]{1,0:T(8,128)(2,1)}) %all-gather.11.cloned.1.call-update) | async-done | bytes 9437200 | tf_op jit(solution)/shard_map/all_gather | solution.py:42
  733.3 12.7 %convert_element_type.101 = f32[1536,3072]{1,0:T(8,128)} convert(bf16[1536,3072]{1,0:T(8,128)(2,1)} %all-gather.11.cloned.1.call-done) | non-fusion elementwise | flops 4718592 | bytes 28311552 | tf_op jit(solution)/shard_map/convert_element_type | solution.py:43
  746.0 69.0 %all-gather.13.cloned.1.call-done = bf16[3072,1536]{0,1:T(8,128)(2,1)} async-done(((bf16[3072,96]{0,1:T(8,128)(2,1)}), bf16[3072,1536]{0,1:T(8,128)(2,1)}) %all-gather.13.cloned.1.call-update) | async-done | bytes 9437200 | tf_op jit(solution)/shard_map/all_gather | solution.py:42
  814.9 13.5 %copy.17 = f32[3072,1536]{1,0:T(8,128)} copy(bf16[3072,1536]{0,1:T(8,128)(2,1)} %all-gather.13.cloned.1.call-done) | data formatting | bytes 28311552
  (96 shorter events, 0.8 us)
Async XLA Ops:
  7.2 13.2 %copy-start.2 = (bf16[1,8,48,768]{3,2,1,0:T(8,128)(2,1)S(1)}, bf16[1,8,48,768]{3,2,1,0:T(8,128)(2,1)}, u32[]{:S(2)}) copy-start(bf16[1,8,48,768]{3,2,1,0:T(8,128)(2,1)} %param.11) | copy-start | bytes 1769476
  7.2 61.6 %all-gather.7.cloned.1.call-start = ((), (), s32[]{:S(2)}) async-start(), calls=%async_computation.4 | async-start | bytes 1769472 | tf_op jit(solution)/shard_map/all_gather | solution.py:29
  8.4 10.1 %collective-permute-start = (bf16[1,3,48,768]{3,2,1,0:T(8,128)(2,1)S(1)}, bf16[1,3,48,768]{3,2,1,0:T(8,128)(2,1)S(1)}, u32[]{:S(2)}, u32[]{:S(2)}) collective-permute-start(bf16[1,3,48,768]{3,2,1,0:T(8,128)(2,1)S(1)} %get-tuple-element.121), channel_id=1, source_target_pairs={{0,2},{2,4},{4,6},{1,3},{3,5},{5,7},{8,10},{10,12},{12,14},{9,11},... | collective-permute-start | bytes 663560 | tf_op jit(solution)/shard_map/ppermute | solution.py:16
  12.4 7.9 collective-permute-start.1
  41.3 27.5 %copy-start.9 = (f32[3072]{0:T(1024)S(1)}, f32[3072]{0:T(1024)}, u32[]{:S(2)}) copy-start(f32[3072]{0:T(1024)} %param.17) | copy-start | bytes 36868
  42.4 87.5 %reduce-scatter.5.cloned.1.call-start = ((), (), s32[]{:S(2)}) async-start(), calls=%async_computation.5 | async-start | bytes 3538944 | tf_op jit(solution)/shard_map/reduce_scatter | solution.py:37
  85.7 1.4 copy-start.3
  94.9 35.0 %copy-start.7 = (f32[768]{0:T(1024)S(1)}, f32[768]{0:T(1024)}, u32[]{:S(2)}) copy-start(f32[768]{0:T(1024)} %param.20) | copy-start | bytes 9220
  94.9 35.0 %copy-start.8 = (f32[768]{0:T(1024)S(1)}, f32[768]{0:T(1024)}, u32[]{:S(2)}) copy-start(f32[768]{0:T(1024)} %param.19) | copy-start | bytes 9220
  94.9 60.7 %all-gather.9.cloned.1.call-start = ((), (), s32[]{:S(2)}) async-start(), calls=%async_computation.6 | async-start | bytes 1769472 | tf_op jit(solution)/shard_map/all_gather | solution.py:29
  132.8 75.4 %reduce-scatter.7.cloned.1.call-start = ((), (), s32[]{:S(2)}) async-start(), calls=%async_computation.7 | async-start | bytes 3538944 | tf_op jit(solution)/shard_map/reduce_scatter | solution.py:37
  164.0 1.4 copy-start.4
  173.2 233.6 %reduce-scatter.9.cloned.1.call-start = ((), (), s32[]{:S(2)}) async-start(), calls=%async_computation.8 | async-start | bytes 20054016 | tf_op jit(solution)/shard_map/reduce_scatter | solution.py:41
  184.4 420.1 %reduce-scatter.11.cloned.1.call-start = ((), (), s32[]{:S(2)}) async-start(), calls=%async_computation.10 | async-start | bytes 20054016 | tf_op jit(solution)/shard_map/reduce_scatter | solution.py:41
  195.9 454.8 %all-gather.15.cloned.1.call-start = ((), (), s32[]{:S(2)}) async-start(), calls=%async_computation.12 | async-start | bytes 2924544 | tf_op jit(solution)/shard_map/all_gather | solution.py:160
  215.5 5.1 copy-start
  224.4 0.7 copy-start.6
  225.1 508.2 %all-gather.11.cloned.1.call-start = ((), (), s32[]{:S(2)}) async-start(), calls=%async_computation.9 | async-start | bytes 10027008 | tf_op jit(solution)/shard_map/all_gather | solution.py:42
  409.0 197.7 %copy-start.1 = (bf16[384,768]{1,0:T(8,128)(2,1)S(1)}, bf16[384,768]{1,0:T(8,128)(2,1)}, u32[]{:S(2)}) copy-start(bf16[384,768]{1,0:T(8,128)(2,1)} %copy-done) | copy-start | bytes 1769476
  409.0 405.9 %all-gather.13.cloned.1.call-start = ((), (), s32[]{:S(2)}) async-start(), calls=%async_computation.11 | async-start | bytes 10027008 | tf_op jit(solution)/shard_map/all_gather | solution.py:42
  606.8 5.6 collective-permute-start.2
  608.6 8.5 %copy-start.5 = (bf16[1,8,48,768]{3,2,1,0:T(8,128)(2,1)S(1)}, bf16[1,8,48,768]{3,2,1,0:T(8,128)(2,1)}, u32[]{:S(2)}) copy-start(bf16[1,8,48,768]{3,2,1,0:T(8,128)(2,1)} %param.21) | copy-start | bytes 1769476
  608.6 8.3 collective-permute-start.3
Sparse Core Ops, SparseCore 0:
  42.5 26.2 all-gather.6
  95.0 34.7 reduce-scatter.4
  132.9 22.7 all-gather.8
  173.3 34.7 reduce-scatter.6
  212.7 194.1 reduce-scatter.8
  411.4 193.1 reduce-scatter.10
  607.4 43.1 all-gather.14
  653.5 79.6 all-gather.10
  735.6 79.3 all-gather.12
